TPU v7x, 768 devices: a whole 4x8x12 slice. The times are simulated.
768 devices in a mesh: space: 192 (over z_hi, y, x, core), orb: 4 (over z_lo).
Axes of the slice: x: 4, y: 8, z: 12 (z_hi: 3, z_lo: 4; z = z_hi * 4 + z_lo), core: 2. Of those that a mesh axis runs over, the one named last changes fastest.
Arguments:
- wavefunctions: float32 [192, 1536, 384], P('space', None, 'orb'), may hold values from -70 to 70
- cell_ham: float32 [192, 4, 729, 729], P('space'), may hold values from -1 to 1, as said below
- cell_nodes: int32 [192, 4, 729], P('space'), may hold values from 0 to 1535, as said below
- cell_count: int32 [192], P('space'), may hold values from 2 to 4, as said below
- upper_nodes: int32 [192, 512], P('space'), may hold values from 0 to 1536, as said below
- lower_nodes: int32 [192, 512], P('space'), may hold values from 0 to 1536, as said below
Outputs:
- rotated: float32 [192, 1536, 384], P('space', 'orb')
Inputs may be any that keep to these rules, and one draw needn't show every extreme that they name: `cell_nodes`: each cell's 729 entries are distinct. `cell_count`: some part has 4 live cells. Entries equal to 1536 are empty slots and come after the live ones; for p < 191, upper_nodes[p, k] is live exactly where lower_nodes[p + 1, k] is, and the two name the same shared node; the live entries of upper_nodes[p] and lower_nodes[p] are all distinct; the last part's list is empty; some list has all 512 slots live. `lower_nodes`: paired with upper_nodes as stated there; the first part's list is empty. `cell_ham`: each cell's matrix is symmetric.
All inputs are finite; a program needn't handle non-finite values.
Results may differ from a plain program's by a relative error of at most 0.0003.
Values sent between devices are 32-bit elements; how exact they have to be, the bound alone decides.
No kernel may reach another device: no remote copies, remote signals or barrier semaphores. Data moves between devices by JAX's collectives and lax.ppermute only.
A program may use at most 64 MiB of HBM per device.

v0:
```python
import jax
import jax.numpy as jnp
from jax import lax
from jax.sharding import PartitionSpec as P

DEGREE = 3


center_shift = 0.5
half_width = 2.0


def shifted(block, axis, distance):
    devices = range(lax.axis_size(axis))
    route = [(i - distance, i) for i in devices if i - distance in devices]
    return lax.ppermute(block, axis, route)


def assemble(nodal_field, matrices, node_map, live_cells):

    def add_cell(cell_slot, assembled):
        rows = lax.dynamic_index_in_dim(node_map, cell_slot, 0, keepdims=False)
        matrix = lax.dynamic_index_in_dim(matrices, cell_slot, 0, keepdims=False)
        product = lax.dot_general(
            matrix,
            jnp.take(nodal_field, rows, axis=0),
            (((0,), (0,)), ((), ())),
            precision=lax.Precision.HIGHEST,
            preferred_element_type=jnp.float32,
        )
        return assembled.at[rows].add(product)

    return lax.fori_loop(0, live_cells, add_cell, jnp.zeros_like(nodal_field))


def share_sums(assembled, upper_list, lower_list):
    outgoing = assembled.at[lower_list].get(mode="fill", fill_value=0.0)
    arriving = shifted(outgoing, "space", -1)
    assembled = assembled.at[upper_list].add(arriving, mode="drop")
    summed = assembled.at[upper_list].get(mode="fill", fill_value=0.0)
    returned = shifted(summed, "space", 1)
    return assembled.at[lower_list].set(returned, mode="drop")


def gram_term(field_rows, node_weight):
    return lax.dot_general(
        field_rows * node_weight[:, None],
        field_rows,
        (((0,), (0,)), ((), ())),
        precision=lax.Precision.HIGHEST,
        preferred_element_type=jnp.float32,
    )


def shards(wavefunctions, cell_ham, cell_nodes, cell_count, upper_nodes, lower_nodes):
    start_field = wavefunctions[0]
    matrices = cell_ham[0]
    node_map = cell_nodes[0]
    live_cells = cell_count[0]
    upper_list = upper_nodes[0]
    lower_list = lower_nodes[0]

    def operate(nodal_field):
        return share_sums(
            assemble(nodal_field, matrices, node_map, live_cells), upper_list, lower_list
        )

    previous = start_field
    current = (operate(start_field) - center_shift * start_field) / half_width
    for repeat in range(DEGREE - 1):
        following = 2.0 * (operate(current) - center_shift * current) / half_width - previous
        previous, current = (current, following)
    node_total = start_field.shape[0]
    weight = jnp.ones((node_total,), jnp.float32).at[lower_list].set(0.0, mode="drop")
    weight = weight * (1.0 / (lax.axis_size("space") * node_total))
    quarter = node_total // lax.axis_size("orb")
    first_node = lax.axis_index("orb") * quarter
    own_rows = lax.all_to_all(current, "orb", split_axis=0, concat_axis=1, tiled=True)
    own_weight = lax.dynamic_slice_in_dim(weight, first_node, quarter)
    gram_total = lax.psum(gram_term(own_rows, own_weight), ("space", "orb"))
    factor = jnp.linalg.cholesky(gram_total)
    rotated = lax.linalg.triangular_solve(
        factor, own_rows, left_side=False, lower=True, transpose_a=True
    )
    return rotated[None]


def solution(mesh):
    in_specs = (
        P("space", None, "orb"),
        P("space", None, None, None),
        P("space", None, None),
        P("space"),
        P("space", None),
        P("space", None),
    )
    out_specs = P("space", "orb", None)
    return jax.shard_map(shards, mesh=mesh, in_specs=in_specs, out_specs=out_specs, check_vma=False)
```

profile of v0, /device:TPU:1, one launch (start us, length us, event | category | flops | bytes accessed | tf_op | source)
XLA Modules:
  0.0 910.8 jit_solution(478002513190622198)
XLA Ops:
  6.5 8.8 copy.26
  15.7 44.0 %while.31 = (s32[]{:T(128)}, f32[1536,96]{1,0:T(8,128)S(1)}, s32[]{:T(128)}, s32[4,729]{1,0:T(4,128)S(1)}, f32[4,729,729]{2,1,0:T(8,128)}, /*index=5*/f32[1536,96]{1,0:T(8,128)S(1)}, s32[]{:T(128)}, s32[]{:T(128)}, s32[]{:T(128)}) while((s32[]{:T(128)}, f32[1536,96]{1,0:T(8,128)S(1)}, s32[]{:T(128)}, s32[4,729]{1,0:T(4,128)S(1)}, ...), condition=%wide.region_2.4_spmd, body=%wide.region_0.3_spmd.sunk | while | flops 612369792 | bytes 4255397 | solution.py:33
  18.2 5.6 fusion.72
  23.8 6.3 scatter_fusion
  32.6 5.6 fusion.72
  38.2 6.3 scatter_fusion
  47.1 5.6 fusion.72
  52.7 6.3 scatter_fusion
  63.0 21.0 %collective-permute-done = f32[512,96]{1,0:T(8,128)S(1)} collective-permute-done((f32[512,96]{1,0:T(8,128)S(1)}, f32[512,96]{1,0:T(8,128)S(1)}, u32[]{:S(2)}, u32[]{:S(2)}) %collective-permute-start) | collective-permute-done | bytes 196640 | tf_op jit(solution)/shard_map/ppermute | solution.py:16
  83.9 4.1 scatter_fusion.3
  91.1 3.3 collective-permute-done.1
  94.4 2.0 scatter_fusion.4
  96.6 47.4 %while.32 = (s32[]{:T(128)}, f32[1536,96]{1,0:T(8,128)S(1)}, s32[]{:T(128)}, s32[4,729]{1,0:T(4,128)S(1)}, f32[4,729,729]{2,1,0:T(8,128)}, /*index=5*/f32[1536,96]{1,0:T(8,128)S(1)}, s32[]{:T(128)}, s32[]{:T(128)}, s32[]{:T(128)}) while((s32[]{:T(128)}, f32[1536,96]{1,0:T(8,128)S(1)}, s32[]{:T(128)}, s32[4,729]{1,0:T(4,128)S(1)}, ...), condition=%wide.region_7.9_spmd, body=%wide.region_5.8_spmd.sunk | while | flops 612369792 | bytes 4255397 | solution.py:33
  99.1 6.3 fusion.76
  105.4 6.7 scatter_fusion.1
  114.6 6.3 fusion.76
  121.0 6.7 scatter_fusion.1
  130.2 6.3 fusion.76
  136.6 6.7 scatter_fusion.1
  147.9 22.1 %collective-permute-done.2 = f32[512,96]{1,0:T(8,128)S(1)} collective-permute-done((f32[512,96]{1,0:T(8,128)S(1)}, f32[512,96]{1,0:T(8,128)S(1)}, u32[]{:S(2)}, u32[]{:S(2)}) %collective-permute-start.2) | collective-permute-done | bytes 196640 | tf_op jit(solution)/shard_map/ppermute | solution.py:16
  169.9 3.6 scatter_fusion.5
  177.4 3.6 collective-permute-done.3
  181.0 2.2 scatter_fusion.6
  184.3 47.3 %while.33 = (s32[]{:T(128)}, f32[1536,96]{1,0:T(8,128)S(1)}, s32[]{:T(128)}, s32[4,729]{1,0:T(4,128)S(1)}, f32[4,729,729]{2,1,0:T(8,128)}, /*index=5*/f32[1536,96]{1,0:T(8,128)}, s32[]{:T(128)}, s32[]{:T(128)}, s32[]{:T(128)}) while((s32[]{:T(128)}, f32[1536,96]{1,0:T(8,128)S(1)}, s32[]{:T(128)}, s32[4,729]{1,0:T(4,128)S(1)}, ...), condition=%wide.region_12.14_spmd, body=%wide.region_10.13_spmd.sunk | while | flops 612369792 | bytes 4255397 | solution.py:33
  185.0 2.9 gather_fusion.2
  187.9 5.6 fusion.80
  193.5 6.3 scatter_fusion.2
  200.6 2.9 gather_fusion.2
  203.4 5.6 fusion.80
  209.1 6.3 scatter_fusion.2
  216.1 2.9 gather_fusion.2
  219.0 5.6 fusion.80
  224.6 6.3 scatter_fusion.2
  234.8 22.0 %collective-permute-done.4 = f32[512,96]{1,0:T(8,128)S(1)} collective-permute-done((f32[512,96]{1,0:T(8,128)S(1)}, f32[512,96]{1,0:T(8,128)S(1)}, u32[]{:S(2)}, u32[]{:S(2)}) %collective-permute-start.4) | collective-permute-done | bytes 196640 | tf_op jit(solution)/shard_map/ppermute | solution.py:16
  256.7 3.6 scatter_fusion.7
  263.5 3.3 collective-permute-done.5
  270.0 7.0 all-to-all-start
  276.9 2.9 scatter_custom_fusion.9
  279.9 12.3 %all-to-all-done = f32[4,384,96]{1,2,0:T(8,128)S(1)} async-done(((f32[4,384,96]{1,2,0:T(8,128)}), f32[4,384,96]{1,2,0:T(8,128)S(1)}, u32[]{:S(2)}, u32[]{:S(2)}) %all-to-all-start) | async-done | bytes 589856 | tf_op jit(solution)/shard_map/all_to_all | solution.py:78
  292.2 2.1 fusion.49
  294.4 508.7 %all-reduce.3.cloned.1.call-done = f32[384,384]{0,1:T(8,128)} async-done(((f32[384,384]{0,1:T(8,128)}), f32[384,384]{0,1:T(8,128)}) %all-reduce.3.cloned.1.call-update) | async-done | bytes 589840 | tf_op jit(solution)/shard_map/psum | solution.py:80
  805.5 11.7 %cholesky.77 = f32[128,128]{1,0:T(8,128)S(1)} custom-call(f32[128,128]{1,0:T(8,128)S(1)} %cholesky.192), custom_call_target="Cholesky" | custom-call | tf_op jit(solution)/shard_map/jit(cholesky)/cholesky | solution.py:81
  817.3 9.8 %custom-call.22 = f32[1,128,128]{1,2,0:T(8,128)S(1)} custom-call(f32[1,128,128]{2,1,0:T(8,128)S(1)} %get-tuple-element.168), custom_call_target="InvertDiagBlocksLowerTriangular" | custom-call | tf_op jit(solution)/shard_map/jit(cholesky)/cholesky | solution.py:81
  827.7 11.7 %cholesky.162 = f32[128,128]{1,0:T(8,128)S(1)} custom-call(f32[128,128]{1,0:T(8,128)S(1)} %cholesky.196), custom_call_target="Cholesky" | custom-call | tf_op jit(solution)/shard_map/jit(cholesky)/cholesky | solution.py:81
  839.5 9.9 %custom-call.23 = f32[1,128,128]{1,2,0:T(8,128)S(1)} custom-call(f32[1,128,128]{2,1,0:T(8,128)S(1)} %get-tuple-element.165), custom_call_target="InvertDiagBlocksLowerTriangular" | custom-call | tf_op jit(solution)/shard_map/jit(cholesky)/cholesky | solution.py:81
  849.9 11.7 %cholesky.181 = f32[128,128]{1,0:T(8,128)S(1)} custom-call(f32[128,128]{1,0:T(8,128)S(1)} %convolution_subtract_fusion.3), custom_call_target="Cholesky" | custom-call | tf_op jit(solution)/shard_map/jit(cholesky)/cholesky | solution.py:81
  865.0 6.4 while.34
  871.3 29.5 %custom-call.24 = f32[3,128,128]{1,2,0:T(8,128)S(1)} custom-call(f32[3,128,128]{2,1,0:T(8,128)S(1)} %get-tuple-element.115), custom_call_target="InvertDiagBlocksLowerTriangular" | custom-call | tf_op jit(solution)/shard_map/triangular_solve | solution.py:82
  (145 shorter events, 50.1 us)
Async XLA Ops:
  6.5 8.8 copy-start.2
  6.5 9.2 %copy-start.1 = (s32[1,4,729]{2,1,0:T(4,128)S(1)}, s32[1,4,729]{2,1,0:T(4,128)}, u32[]{:S(2)}) copy-start(s32[1,4,729]{2,1,0:T(4,128)} %param.16) | copy-start | bytes 34996
  15.7 44.0 %copy-start.9 = (s32[1,512]{1,0:T(1,128)S(1)}, s32[1,512]{1,0:T(1,128)}, u32[]{:S(2)}) copy-start(s32[1,512]{1,0:T(1,128)} %param.19) | copy-start | bytes 6148
  15.7 47.2 %copy-start.10 = (s32[1,512]{1,0:T(1,128)S(1)}, s32[1,512]{1,0:T(1,128)}, u32[]{:S(2)}) copy-start(s32[1,512]{1,0:T(1,128)} %param.18) | copy-start | bytes 6148
  59.7 36.9 %copy-start.3 = (s32[1024]{0:T(1024)}, s32[1024]{0:T(1024)S(1)}, u32[]{:S(2)}) copy-start(s32[1024]{0:T(1024)S(1)} %pad_clamp_fusion.4) | copy-start | bytes 12292
  59.8 3.2 copy-start.7
  61.0 23.0 %collective-permute-start = (f32[512,96]{1,0:T(8,128)S(1)}, f32[512,96]{1,0:T(8,128)S(1)}, u32[]{:S(2)}, u32[]{:S(2)}) collective-permute-start(f32[512,96]{1,0:T(8,128)S(1)} %broadcast_select_fusion.5), channel_id=1, source_target_pairs={{4,0},{8,4},{12,8},{16,12},{20,16},{24,20},{28,24},{32,28},{36,32}... | collective-permute-start | bytes 589832 | tf_op jit(solution)/shard_map/ppermute | solution.py:16
  62.9 31.5 %copy-start.5 = (pred[512]{0:T(512)(128)(4,1)}, pred[512]{0:T(512)(128)(4,1)S(1)}, u32[]{:S(2)}) copy-start(pred[512]{0:T(512)(128)(4,1)S(1)} %compare_and_fusion.3) | copy-start | bytes 1540
  89.2 5.2 collective-permute-start.1
  144.0 30.6 %copy-start.6 = (pred[512]{0:T(512)(128)(4,1)S(1)}, pred[512]{0:T(512)(128)(4,1)}, u32[]{:S(2)}) copy-start(pred[512]{0:T(512)(128)(4,1)} %copy-done.5) | copy-start | bytes 1540
  145.9 24.0 %collective-permute-start.2 = (f32[512,96]{1,0:T(8,128)S(1)}, f32[512,96]{1,0:T(8,128)S(1)}, u32[]{:S(2)}, u32[]{:S(2)}) collective-permute-start(f32[512,96]{1,0:T(8,128)S(1)} %broadcast_select_fusion.3), channel_id=1, source_target_pairs={{4,0},{8,4},{12,8},{16,12},{20,16},{24,20},{28,24},{32,28},{36,32}... | collective-permute-start | bytes 589832 | tf_op jit(solution)/shard_map/ppermute | solution.py:16
  175.4 5.5 collective-permute-start.3
  184.3 47.4 %copy-start.4 = (s32[1024]{0:T(1024)S(1)}, s32[1024]{0:T(1024)}, u32[]{:S(2)}) copy-start(s32[1024]{0:T(1024)} %copy-done.3) | copy-start | bytes 12292
  184.3 48.4 %copy-start.8 = (pred[512]{0:T(512)(128)(4,1)S(1)}, pred[512]{0:T(512)(128)(4,1)}, u32[]{:S(2)}) copy-start(pred[512]{0:T(512)(128)(4,1)} %copy-done.7) | copy-start | bytes 1540
  231.6 37.1 %copy-start = (f32[1536,96]{1,0:T(8,128)S(1)}, f32[1536,96]{1,0:T(8,128)}, u32[]{:S(2)}) copy-start(f32[1536,96]{1,0:T(8,128)} %get-tuple-element.415) | copy-start | bytes 1769476
  232.8 23.9 %collective-permute-start.4 = (f32[512,96]{1,0:T(8,128)S(1)}, f32[512,96]{1,0:T(8,128)S(1)}, u32[]{:S(2)}, u32[]{:S(2)}) collective-permute-start(f32[512,96]{1,0:T(8,128)S(1)} %broadcast_select_fusion.1), channel_id=1, source_target_pairs={{4,0},{8,4},{12,8},{16,12},{20,16},{24,20},{28,24},{32,28},{36,32}... | collective-permute-start | bytes 589832 | tf_op jit(solution)/shard_map/ppermute | solution.py:16
  261.5 5.2 collective-permute-start.5
  270.0 22.2 %all-to-all-start = ((f32[4,384,96]{1,2,0:T(8,128)}), f32[4,384,96]{1,2,0:T(8,128)S(1)}, u32[]{:S(2)}, u32[]{:S(2)}) async-start(f32[4,384,96]{1,2,0:T(8,128)} %copy.17), calls=%async_computation | async-start | bytes 1179648 | tf_op jit(solution)/shard_map/all_to_all | solution.py:78
  276.9 526.2 %all-reduce.3.cloned.1.call-start = ((), (), s32[]{:S(2)}) async-start(), calls=%async_computation.1 | async-start | bytes 1179648 | tf_op jit(solution)/shard_map/psum | solution.py:80
Sparse Core Ops, SparseCore 0:
  294.5 508.5 all-reduce.2
where the time goes:
time: 921 us; the launch traced here: 911 us
  waiting for transfers between devices  596 us (65%)
  other arithmetic  161 us (17%)
  matrix products  57.4 us (6%)
  local copies, waits for them, and re-layouts  53.5 us (6%)
  starting transfers between devices  18.5 us (2%)
  between operations  16.1 us (2%)
    psum x1, waiting for transfers between devices, shards(): gram_total = lax.psum(gram_term(own_rows, own_weight), ('space', 'orb'))  509 us
    ppermute x6, waiting for transfers between devices, shifted(): return lax.ppermute(block, axis, route)  75.2 us
    scatter-add x9, other arithmetic, add_cell(): return assembled.at[rows].add(product)  58.3 us
    another operation x10, other arithmetic, shards(): factor = jnp.linalg.cholesky(gram_total)  56.3 us
    dot_general x9, matrix products, add_cell(): lax.dot_general(matrix, jnp.take(nodal_field, rows, axis=0), (((0,), (0,)...  52.5 us
    another operation x3, other arithmetic, shards(): lax.linalg.triangular_solve(factor, own_rows, left_side=False, lower=True...  29.5 us
    gather x9, local copies, waits for them, and re-layouts, add_cell(): jnp.take(nodal_field, rows, axis=0)  18.9 us
  transfers between devices with their start and end apart: 8, of which 8 were waited for; matrix products, arithmetic and copies ran while one was open for 0% of the time, Pallas kernels for 0%

commit v1 on v0

v1 whole, which is shorter than its diff:
```python
import functools

import jax
import jax.numpy as jnp
from jax import lax
from jax.experimental import pallas as pl
from jax.experimental.pallas import tpu as pltpu
from jax.sharding import Mesh, PartitionSpec as P

DEGREE = 3
CAP = 4
CELL = 729
NODES = 1536
ROWS = 1544
COLS = 384
OWN = 96
SHARE = 512
BLK = 128

center_shift = 0.5
half_width = 2.0

SPACE = ("z_hi", "y", "x", "core")
NEAR = ("x", "core", "orb")
FAR = ("z_hi", "y")

F32 = jnp.float32
BF16 = jnp.bfloat16
NT = (((1,), (1,)), ((), ()))
NN = (((1,), (0,)), ((), ()))
TN = (((0,), (0,)), ((), ()))
VMEM_BYTES = 56 * 1024 * 1024


def halves(value):
    high = value.astype(BF16)
    low = (value - high.astype(F32)).astype(BF16)
    return high, low


def dot(a, b, dims):
    return lax.dot_general(a, b, dims, preferred_element_type=F32)


def dot_exact(a, b, dims):
    return lax.dot_general(a, b, dims, precision=lax.Precision.HIGHEST, preferred_element_type=F32)


def dot_three(a, b, dims):
    a_high, a_low = halves(a)
    b_high, b_low = halves(b)
    return dot(a_high, b_high, dims) + (dot(a_high, b_low, dims) + dot(a_low, b_high, dims))


def add_rims(field, list_ref, arrived, scale):
    step = 16

    def some(i, carry):
        first = i * step
        picks = [list_ref[first + j] for j in range(step)]
        new = [field[pl.ds(picks[j], 1), :] + arrived[pl.ds(first + j, 1), :] * scale for j in range(step)]
        for j in range(step):
            field[pl.ds(picks[j], 1), :] = new[j]
        return carry

    lax.fori_loop(0, SHARE // step, some, 0)


def take_rims(field, list_ref, out):
    step = 16

    def some(i, carry):
        first = i * step
        rows = [field[pl.ds(list_ref[first + j], 1), :] for j in range(step)]
        for j in range(step):
            out[pl.ds(first + j, 1), :] = rows[j]
        return carry

    lax.fori_loop(0, SHARE // step, some, 0)


def take_cell(field, nodes_ref, cell, out):
    step = 27

    def some(i, carry):
        first = i * step
        rows = [field[pl.ds(nodes_ref[cell * CELL + first + j], 1), :] for j in range(step)]
        for j in range(step):
            out[pl.ds(first + j, 1), :] = rows[j]
        return carry

    lax.fori_loop(0, CELL // step, some, 0)


def add_cell(total, nodes_ref, cell, product):
    step = 27

    def some(i, carry):
        first = i * step
        picks = [nodes_ref[cell * CELL + first + j] for j in range(step)]
        new = [total[pl.ds(picks[j], 1), :] + product[pl.ds(first + j, 1), :] for j in range(step)]
        for j in range(step):
            total[pl.ds(picks[j], 1), :] = new[j]
        return carry

    lax.fori_loop(0, CELL // step, some, 0)


def cell_work(cell, nodes_ref, high, low, field, total, gathered, packed, product):
    take_cell(field, nodes_ref, cell, gathered)
    rows = gathered[0:CELL, :]
    rows_high, rows_low = halves(rows)
    packed[:, 0:BLK] = rows_high
    packed[:, BLK:] = rows_low
    both = dot(high[...], packed[...], NN)
    rest = dot(low[...], packed[:, 0:BLK], NN)
    product[0:CELL, :] = both[:, 0:BLK] + (both[:, BLK:] + rest)
    add_cell(total, nodes_ref, cell, product)


def finish_step(field, total, previous, scale, upper_ref, lower_ref, next_out, up_out, low_out):
    step = total[0:NODES, :] - center_shift * field[0:NODES, :]
    step = step * scale
    if previous is not None:
        step = step - previous
    next_out[...] = step
    take_rims(total, upper_ref, up_out)
    take_rims(total, lower_ref, low_out)


def first_kernel(live_ref, nodes_ref, upper_ref, lower_ref, start_ref, ham_ref, next_out, up_out, low_out, high_out, low_part_out, field, total, gathered, packed, product):
    cell = pl.program_id(0)

    @pl.when(cell == 0)
    def _():
        field[...] = jnp.zeros_like(field)
        field[0:NODES, 0:OWN] = start_ref[0]
        total[...] = jnp.zeros_like(total)

    @pl.when(cell < live_ref[0])
    def _():
        high, low = halves(ham_ref[0, 0])
        high_out[0] = high
        low_part_out[0] = low
        cell_work(cell, nodes_ref, high_out.at[0], low_part_out.at[0], field, total, gathered, packed, product)

    @pl.when(cell == CAP - 1)
    def _():
        finish_step(field, total, None, 1.0 / half_width, upper_ref, lower_ref, next_out, up_out, low_out)


def next_kernel(first, live_ref, nodes_ref, upper_ref, lower_ref, part_ref, prev_ref, from_above_ref, from_below_ref, high_ref, low_ref, field_out, next_out, up_out, low_out, total, gathered, packed, product):
    cell = pl.program_id(0)

    @pl.when(cell == 0)
    def _():
        scale = 1.0 / half_width if first else 1.0
        field_out[0:NODES, :] = part_ref[...]
        field_out[NODES:, :] = jnp.zeros((ROWS - NODES, BLK), F32)
        add_rims(field_out, upper_ref, from_above_ref, scale)
        add_rims(field_out, lower_ref, from_below_ref, scale)
        field_out[NODES:, :] = jnp.zeros((ROWS - NODES, BLK), F32)
        total[...] = jnp.zeros_like(total)

    @pl.when(cell < live_ref[0])
    def _():
        cell_work(cell, nodes_ref, high_ref.at[0], low_ref.at[0], field_out, total, gathered, packed, product)

    @pl.when(cell == CAP - 1)
    def _():
        if first:
            previous = jnp.concatenate([prev_ref[0], jnp.zeros((NODES, BLK - OWN), F32)], axis=1)
        else:
            previous = prev_ref[0:NODES, :]
        finish_step(field_out, total, previous, 1.0, upper_ref, lower_ref, next_out, up_out, low_out)


def last_kernel(upper_ref, lower_ref, part_ref, from_above_ref, from_below_ref, out, weight_out, field, weight):
    field[0:NODES, :] = part_ref[...]
    field[NODES:, :] = jnp.zeros((ROWS - NODES, BLK), F32)
    add_rims(field, upper_ref, from_above_ref, 1.0)
    add_rims(field, lower_ref, from_below_ref, 1.0)
    out[...] = field[0:NODES, 0:OWN]
    weight[...] = jnp.full((ROWS, BLK), 1.0 / (192 * NODES), F32)
    nothing = jnp.zeros((1, BLK), F32)

    def some(i, carry):
        for j in range(16):
            weight[pl.ds(lower_ref[i * 16 + j], 1), :] = nothing
        return carry

    lax.fori_loop(0, SHARE // 16, some, 0)
    weight_out[...] = weight[0:NODES, :]


def gram_kernel(quarter_ref, own_ref, weight_ref, rows_out, gram_out):
    del quarter_ref
    rows = jnp.concatenate([own_ref[0], own_ref[1], own_ref[2], own_ref[3]], axis=1)
    rows_out[...] = rows
    w = weight_ref[...]
    left = jnp.concatenate([rows[:, 0:128] * w, rows[:, 128:256] * w, rows[:, 256:384] * w], axis=1).T
    left_high, left_low = halves(left)
    right_high, right_low = halves(rows)

    def block_row(k):
        a_high, a_low = left_high[k * BLK:(k + 1) * BLK], left_low[k * BLK:(k + 1) * BLK]
        b_high, b_low = right_high[:, :(k + 1) * BLK], right_low[:, :(k + 1) * BLK]
        return dot(a_high, b_high, NN) + (dot(a_high, b_low, NN) + dot(a_low, b_high, NN))

    first, second, third = block_row(0), block_row(1), block_row(2)
    blocks = [first, second[:, :BLK], third[:, :BLK], second[:, BLK:], third[:, BLK:2 * BLK], third[:, 2 * BLK:]]
    for k, block in enumerate(blocks):
        gram_out[k * BLK:(k + 1) * BLK, :] = block


def inverse_factor(work, inverse):
    lane = lax.broadcasted_iota(jnp.int32, (8, BLK), 0)

    def panel(p, carry):
        first = pl.multiple_of(p * 8, 8)
        panel_a = work[pl.ds(first, 8), 0:BLK]
        panel_i = work[pl.ds(first, 8), BLK:]
        turned = pltpu.roll(panel_a, jnp.where(p == 0, 0, BLK - first), 1)
        columns = [jnp.broadcast_to(turned[:, k:k + 1], (8, BLK)) for k in range(8)]
        e = {(i, k): jnp.broadcast_to(columns[k][i:i + 1, :], (8, BLK)) for i in range(8) for k in range(i + 1)}
        rows_a = [jnp.broadcast_to(panel_a[i:i + 1, :], (8, BLK)) for i in range(8)]
        rows_i = [jnp.broadcast_to(panel_i[i:i + 1, :], (8, BLK)) for i in range(8)]
        for k in range(8):
            pivot = e[k, k]
            r = lax.rsqrt(pivot)
            r = r * (1.5 - 0.5 * pivot * r * r)
            rows_a[k] = rows_a[k] * r
            rows_i[k] = rows_i[k] * r
            below = {i: e[i, k] * r for i in range(k + 1, 8)}
            for i in range(k + 1, 8):
                for j in range(k + 1, i + 1):
                    e[i, j] = e[i, j] - below[i] * below[j]
                rows_a[i] = rows_a[i] - below[i] * rows_a[k]
                rows_i[i] = rows_i[i] - below[i] * rows_i[k]
        new_a, new_i = rows_a[0], rows_i[0]
        for k in range(1, 8):
            new_a = jnp.where(lane == k, rows_a[k], new_a)
            new_i = jnp.where(lane == k, rows_i[k], new_i)
        inverse[pl.ds(first, 8), :] = new_i
        both = jnp.concatenate([new_a, new_i], axis=1)

        def three(v):
            v1 = v.astype(BF16).astype(F32)
            rest = v - v1
            v2 = rest.astype(BF16).astype(F32)
            return v1, v2, rest - v2

        a1, a2, a3 = three(new_a)
        b1, b2, b3 = three(both)
        left = jnp.concatenate([a1, a1, a2, a1, a2, a3], axis=0).astype(BF16)
        right = jnp.concatenate([b1, b2, b1, b3, b2, b1], axis=0).astype(BF16)
        work[...] = work[...] - dot(left, right, TN)
        return carry

    lax.fori_loop(0, BLK // 8, panel, 0)


def rotate_kernel(gram_ref, rows_ref, out, work, inverse):
    eye = (lax.broadcasted_iota(jnp.int32, (BLK, BLK), 0) == lax.broadcasted_iota(jnp.int32, (BLK, BLK), 1)).astype(F32)

    def factor(block):
        work[:, 0:BLK] = block
        work[:, BLK:] = eye
        inverse_factor(work, inverse)
        return inverse[...]

    m1 = factor(gram_ref[0:BLK, :])
    left = dot_exact(gram_ref[BLK:3 * BLK, :], m1, NT)
    l21, l31 = left[0:BLK], left[BLK:]
    rows = rows_ref[...]
    z1 = dot_three(rows[:, 0:BLK], m1, NT)
    out[0, :, 0:BLK] = z1
    m2 = factor(gram_ref[3 * BLK:4 * BLK, :] - dot_exact(l21, l21, NT))
    l32 = dot_exact(gram_ref[4 * BLK:5 * BLK, :] - dot_exact(l31, l21, NT), m2, NT)
    z2 = dot_three(rows[:, BLK:2 * BLK] - dot_three(z1, l21, NT), m2, NT)
    out[0, :, BLK:2 * BLK] = z2
    m3 = factor(gram_ref[5 * BLK:, :] - dot_exact(l31, l31, NT) - dot_exact(l32, l32, NT))
    z3 = dot_three(rows[:, 2 * BLK:] - dot_three(z1, l31, NT) - dot_three(z2, l32, NT), m3, NT)
    out[0, :, 2 * BLK:] = z3


def smem():
    return pl.BlockSpec(memory_space=pltpu.SMEM)


def whole(*shape):
    return pl.BlockSpec(shape, lambda *_: (0,) * len(shape))


def params():
    return pltpu.CompilerParams(vmem_limit_bytes=VMEM_BYTES)


def scratch(with_field):
    field = [pltpu.VMEM((ROWS, BLK), F32)] if with_field else []
    return field + [
        pltpu.VMEM((ROWS, BLK), F32),
        pltpu.VMEM((736, BLK), F32),
        pltpu.VMEM((CELL, 2 * BLK), BF16),
        pltpu.VMEM((736, BLK), F32),
    ]


def struct(*shape, dtype=F32):
    return jax.ShapeDtypeStruct(shape, dtype)


def first_step(live, nodes, upper, lower, start, ham):
    cell_block = pl.BlockSpec((1, CELL, CELL), lambda c: (c, 0, 0))
    return pl.pallas_call(
        first_kernel,
        grid=(CAP,),
        in_specs=[smem(), smem(), smem(), smem(), whole(1, NODES, OWN), pl.BlockSpec((1, 1, CELL, CELL), lambda c: (0, c, 0, 0))],
        out_specs=[whole(NODES, BLK), whole(SHARE, BLK), whole(SHARE, BLK), cell_block, cell_block],
        out_shape=[struct(NODES, BLK), struct(SHARE, BLK), struct(SHARE, BLK), struct(CAP, CELL, CELL, dtype=BF16), struct(CAP, CELL, CELL, dtype=BF16)],
        scratch_shapes=scratch(True),
        compiler_params=params(),
        name="first_step",
    )(live, nodes, upper, lower, start, ham)


def next_step(first, live, nodes, upper, lower, part, previous, above, below, high, low):
    cell_block = pl.BlockSpec((1, CELL, CELL), lambda c: (c, 0, 0))
    return pl.pallas_call(
        functools.partial(next_kernel, first),
        grid=(CAP,),
        in_specs=[smem(), smem(), smem(), smem(), whole(NODES, BLK), whole(*previous.shape), whole(SHARE, BLK), whole(SHARE, BLK), cell_block, cell_block],
        out_specs=[whole(ROWS, BLK), whole(NODES, BLK), whole(SHARE, BLK), whole(SHARE, BLK)],
        out_shape=[struct(ROWS, BLK), struct(NODES, BLK), struct(SHARE, BLK), struct(SHARE, BLK)],
        scratch_shapes=scratch(False),
        compiler_params=params(),
        name="second_step" if first else "third_step",
    )(live, nodes, upper, lower, part, previous, above, below, high, low)


def last_step(upper, lower, part, above, below):
    return pl.pallas_call(
        last_kernel,
        in_specs=[smem(), smem()] + [pl.BlockSpec(memory_space=pltpu.VMEM)] * 3,
        out_specs=[pl.BlockSpec(memory_space=pltpu.VMEM)] * 2,
        out_shape=[struct(NODES, OWN), struct(NODES, BLK)],
        scratch_shapes=[pltpu.VMEM((ROWS, BLK), F32)] * 2,
        compiler_params=params(),
        name="last_step",
    )(upper, lower, part, above, below)


def gram_step(quarter, own, weight):
    return pl.pallas_call(
        gram_kernel,
        grid_spec=pltpu.PrefetchScalarGridSpec(
            num_scalar_prefetch=1,
            grid=(1,),
            in_specs=[whole(4, COLS, OWN), pl.BlockSpec((COLS, BLK), lambda i, q: (q[0], 0))],
            out_specs=[whole(COLS, COLS), whole(6 * BLK, BLK)],
        ),
        out_shape=[struct(COLS, COLS), struct(6 * BLK, BLK)],
        compiler_params=params(),
        name="gram_step",
    )(quarter, own, weight)


def rotate_step(gram, rows):
    return pl.pallas_call(
        rotate_kernel,
        out_shape=struct(1, COLS, COLS),
        scratch_shapes=[pltpu.VMEM((BLK, 2 * BLK), F32), pltpu.VMEM((BLK, BLK), F32)],
        compiler_params=params(),
        name="rotate_step",
    )(gram, rows)


def exchange(up, low):
    last = 191
    from_above = lax.ppermute(low, SPACE, [(i + 1, i) for i in range(last)])
    from_below = lax.ppermute(up, SPACE, [(i, i + 1) for i in range(last)])
    return from_above, from_below


def scatter_sum(value, axes):
    parts = lax.axis_size(axes)
    pieces = lax.all_to_all(value.reshape(parts, -1, BLK), axes, 0, 0, tiled=True)
    return pieces.sum(0)


def total_sum(value, axes):
    parts = lax.axis_size(axes)
    copies = jnp.broadcast_to(value[None], (parts,) + value.shape)
    return lax.all_to_all(copies, axes, 0, 0, tiled=True).sum(0)


def spread(value, axes):
    parts = lax.axis_size(axes)
    copies = jnp.broadcast_to(value[None], (parts,) + value.shape)
    return lax.all_to_all(copies, axes, 0, 0, tiled=True).reshape(-1, BLK)


def shards(wavefunctions, cell_ham, cell_nodes, cell_count, upper_nodes, lower_nodes):
    nodes = cell_nodes.reshape(-1)
    upper = upper_nodes.reshape(-1)
    lower = lower_nodes.reshape(-1)
    part, up, low, ham_high, ham_low = first_step(cell_count, nodes, upper, lower, wavefunctions, cell_ham)
    above, below = exchange(up, low)
    previous = wavefunctions
    for repeat in range(DEGREE - 1):
        current, part, up, low = next_step(repeat == 0, cell_count, nodes, upper, lower, part, previous, above, below, ham_high, ham_low)
        above, below = exchange(up, low)
        previous = current
    filtered, weight = last_step(upper, lower, part, above, below)
    own = lax.all_to_all(filtered.reshape(4, COLS, OWN), "orb", 0, 0, tiled=True)
    quarter = lax.axis_index("orb").astype(jnp.int32).reshape(1)
    rows, gram = gram_step(quarter, own, weight)
    gram = spread(total_sum(scatter_sum(gram, NEAR), FAR), NEAR)
    return rotate_step(gram, rows)


def solution(mesh):
    fine = Mesh(mesh.devices.reshape(3, 8, 4, 2, 4), SPACE + ("orb",))
    in_specs = (
        P(SPACE, None, "orb"),
        P(SPACE, None, None, None),
        P(SPACE, None, None),
        P(SPACE),
        P(SPACE, None),
        P(SPACE, None),
    )
    out_specs = P(SPACE, "orb", None)
    return jax.shard_map(shards, mesh=fine, in_specs=in_specs, out_specs=out_specs, check_vma=False)
```

time: 921 us -> 266 us (0.29); the launches traced: 911 us -> 266 us
  waiting for transfers between devices: 596 us -> 27.5 us
  other arithmetic: 161 us -> 0.07 us
  blocking collectives: 0 us -> 110 us
  Pallas kernels: 0 us -> 76.9 us
  matrix products: 57.4 us -> 0 us
  local copies, waits for them, and re-layouts: 53.5 us -> 17.9 us
  between operations: 16.1 us -> 0.76 us
  starting transfers between devices: 18.5 us -> 32.8 us
    psum x1 -> x0, waiting for transfers between devices: 509 us -> none  [shards(): gram_total = lax.psum(gram_term(own_rows, own_weight), ('space', 'orb'))]
    all_to_all x0 -> x3, blocking collectives: none -> 110 us  [the longest x1 68.9 us: total_sum(): return lax.all_to_all(copies, axes, 0, 0, tiled=True).sum(0)]
    another operation x13 -> x0, other arithmetic: 85.9 us -> none  [the longest x10 56.3 us: shards(): factor = jnp.linalg.cholesky(gram_total)]
    pallas_call x0 -> x6, Pallas kernels: none -> 76.9 us  [the longest x2 27.8 us: next_step(): pl.pallas_call(functools.partial(next_kernel, first), grid=(CAP,), in_spe...]
    scatter-add x12 -> x0, other arithmetic: 69.6 us -> none  [the longest x9 58.3 us: add_cell(): return assembled.at[rows].add(product)]
    ppermute x6, waiting for transfers between devices: 75.2 us -> 10.8 us  [the longest x3 6.16 us: exchange(): from_below = lax.ppermute(up, SPACE, [(i, i + 1) for i in range(last)])]
    dot_general x10 -> x0, matrix products: 54.6 us -> none  [the longest x9 52.5 us: add_cell(): lax.dot_general(matrix, jnp.take(nodal_field, rows, axis=0), (((0,), (0,)...]
    gather x15 -> x0, local copies, waits for them, and re-layouts: 25.3 us -> none  [the longest x9 18.9 us: add_cell(): jnp.take(nodal_field, rows, axis=0)]
  transfers between devices with their start and end apart: 8 -> 7, of which waited for: 8 -> 6; matrix products, arithmetic and copies ran while one was open for 0% -> 0% of each run, Pallas kernels for 0% -> 0%
where the time goes in v1:
time: 266 us
  blocking collectives  110 us (41%)
  Pallas kernels  76.9 us (29%)
  starting transfers between devices  32.8 us (12%)
  waiting for transfers between devices  27.5 us (10%)
  local copies, waits for them, and re-layouts  17.9 us (7%)
    all_to_all x1, blocking collectives, total_sum(): return lax.all_to_all(copies, axes, 0, 0, tiled=True).sum(0)  68.9 us
    pallas_call x2, Pallas kernels, next_step(): pl.pallas_call(functools.partial(next_kernel, first), grid=(CAP,), in_spe...  27.8 us
    pallas_call x1, Pallas kernels, rotate_step(): pl.pallas_call(rotate_kernel, out_shape=struct(1, COLS, COLS), scratch_sh...  26.9 us
    all_to_all x1, blocking collectives, scatter_sum(): lax.all_to_all(value.reshape(parts, -1, BLK), axes, 0, 0, tiled=True)  20.7 us
    all_to_all x1, blocking collectives, spread(): return lax.all_to_all(copies, axes, 0, 0, tiled=True).reshape(-1, BLK)  20.4 us
    all_to_all x1, waiting for transfers between devices, shards(): lax.all_to_all(filtered.reshape(4, COLS, OWN), 'orb', 0, 0, tiled=True)  16.7 us
    ppermute x3, starting transfers between devices, exchange(): from_above = lax.ppermute(low, SPACE, [(i + 1, i) for i in range(last)])  16.2 us
    pallas_call x1, Pallas kernels, first_step(): pl.pallas_call(first_kernel, grid=(CAP,), in_specs=[smem(), smem(), smem(...  14.7 us
  transfers between devices with their start and end apart: 7, of which 6 were waited for; matrix products, arithmetic and copies ran while one was open for 0% of the time, Pallas kernels for 0%

profile of v1, /device:TPU:1, one launch (start us, length us, event | category | flops | bytes accessed | tf_op | source)
XLA Modules:
  0.0 266.0 jit_solution(8465680159171595598)
XLA Ops:
  0.0 1.4 reshape.26.nodes_ref
  2.0 2.2 copy.15.start_ref.prev_ref
  4.3 8.8 %copy.16.ham_ref = f32[1,4,729,729]{3,2,1,0:T(8,128)} copy(f32[1,4,729,729]{3,1,2,0:T(4,128)} %param.7) | data formatting | bytes 17006112 | tf_op args[1]
  13.0 14.7 %first_step.1 = (f32[1536,128]{1,0:T(8,128)}, f32[512,128]{1,0:T(8,128)}, f32[512,128]{1,0:T(8,128)}, bf16[4,729,729]{2,1,0:T(8,128)(2,1)}, bf16[4,729,729]{2,1,0:T(8,128)(2,1)}) custom-call(s32[1]{0:T(128)S(6)} %copy.20.live_ref, s32[2916]{0:T(1024)} %reshape.26.nodes_ref, s32[512]{0:T(512)} %bitcast.9, s32[512]{0:T(512)} %bitcast.13, ...), custom_call_target="tpu_custom_call" | custom-call | tf_op jit(solution)/shard_map/first_step/pallas_call | solution.py:315
  27.8 12.4 %collective-permute-start = (f32[512,128]{1,0:T(8,128)}, f32[512,128]{1,0:T(8,128)S(1)}, u32[]{:S(2)}, u32[]{:S(2)}) collective-permute-start(f32[512,128]{1,0:T(8,128)} %get-tuple-element.22), channel_id=1, source_target_pairs={{4,0},{8,4},{12,8},{16,12},{20,16},{24,20},{28,24},{32,28},{36,32}... | collective-permute-start | bytes 786440 | tf_op jit(solution)/shard_map/ppermute | solution.py:380
  40.2 1.9 collective-permute-start.1
  42.1 0.0 collective-permute-done.from_above_ref
  42.1 0.0 copy-start
  42.1 3.6 %collective-permute-done.1.from_below_ref = f32[512,128]{1,0:T(8,128)S(1)} collective-permute-done((f32[512,128]{1,0:T(8,128)}, f32[512,128]{1,0:T(8,128)S(1)}, u32[]{:S(2)}, u32[]{:S(2)}) %collective-permute-start.1) | collective-permute-done | bytes 262176 | tf_op jit(solution)/shard_map/ppermute | solution.py:381
  45.7 0.0 copy-start.1
  45.7 0.0 copy-done
  45.7 0.7 copy-done.1
  46.4 13.9 %second_step.1 = (f32[1544,128]{1,0:T(8,128)}, f32[1536,128]{1,0:T(8,128)}, f32[512,128]{1,0:T(8,128)}, f32[512,128]{1,0:T(8,128)}) custom-call(s32[1]{0:T(128)S(6)} %copy.20.live_ref, s32[2916]{0:T(1024)} %reshape.26.nodes_ref, s32[512]{0:T(512)} %bitcast.10, s32[512]{0:T(512)} %bitcast.14, f32[1536,128]{1,0:T(8,128)} %get-tuple-element.21.part_ref, ...), custom_call_target="tpu_custom_call" | custom-call | tf_op jit(solution)/shard_map/second_step/pallas_call | solution.py:329
  60.4 1.9 collective-permute-start.2
  62.3 5.6 %collective-permute-start.3 = (f32[512,128]{1,0:T(8,128)}, f32[512,128]{1,0:T(8,128)S(1)}, u32[]{:S(2)}, u32[]{:S(2)}) collective-permute-start(f32[512,128]{1,0:T(8,128)} %get-tuple-element.29), channel_id=1, source_target_pairs={{0,4},{4,8},{8,12},{12,16},{16,20},{20,24},{24,28},{28,32},{32,36}... | collective-permute-start | bytes 786440 | tf_op jit(solution)/shard_map/ppermute | solution.py:381
  67.9 2.3 collective-permute-done.2.from_above_ref
  70.2 0.0 copy-start.4
  70.2 1.3 collective-permute-done.3.from_below_ref
  71.5 0.0 copy-start.5
  71.5 0.0 copy-done.4
  71.5 0.7 copy-done.5
  72.2 13.9 %third_step.1 = (f32[1544,128]{1,0:T(8,128)}, f32[1536,128]{1,0:T(8,128)}, f32[512,128]{1,0:T(8,128)}, f32[512,128]{1,0:T(8,128)}) custom-call(s32[1]{0:T(128)S(6)} %copy.20.live_ref, s32[2916]{0:T(1024)} %reshape.26.nodes_ref, s32[512]{0:T(512)} %bitcast.11, s32[512]{0:T(512)} %bitcast.15, f32[1536,128]{1,0:T(8,128)} %get-tuple-element.26.part_ref, ...), custom_call_target="tpu_custom_call" | custom-call | tf_op jit(solution)/shard_map/third_step/pallas_call | solution.py:329
  86.1 1.9 collective-permute-start.4
  88.0 5.6 %collective-permute-start.5 = (f32[512,128]{1,0:T(8,128)}, f32[512,128]{1,0:T(8,128)S(1)}, u32[]{:S(2)}, u32[]{:S(2)}) collective-permute-start(f32[512,128]{1,0:T(8,128)} %get-tuple-element.32), channel_id=1, source_target_pairs={{0,4},{4,8},{8,12},{12,16},{16,20},{20,24},{24,28},{28,32},{32,36}... | collective-permute-start | bytes 786440 | tf_op jit(solution)/shard_map/ppermute | solution.py:381
  93.6 2.3 collective-permute-done.4.from_above_ref
  95.9 0.0 copy-start.2
  95.9 1.3 collective-permute-done.5.from_below_ref
  97.2 0.0 copy-start.3
  97.2 0.0 copy-done.2
  97.2 0.7 copy-done.3
  97.9 4.8 %last_step.1 = (f32[1536,96]{1,0:T(8,128)}, f32[1536,128]{1,0:T(8,128)}) custom-call(s32[512]{0:T(512)} %bitcast.12, s32[512]{0:T(512)} %bitcast.16, f32[1536,128]{1,0:T(8,128)} %get-tuple-element.30.part_ref, f32[512,128]{1,0:T(8,128)} %copy-done.2, f32[512,128]{1,0:T(8,128)} %copy-done.3), custom_call_target="tpu_custom_call" | custom-call | tf_op jit(solution)/shard_map/last_step/pallas_call | solution.py:342
  102.7 2.2 copy.18
  104.9 3.5 %all-to-all-start = ((f32[4,384,96]{1,2,0:T(8,128)}), f32[4,384,96]{1,2,0:T(8,128)S(1)}, u32[]{:S(2)}, u32[]{:S(2)}) async-start(f32[4,384,96]{1,2,0:T(8,128)} %copy.18), calls=%async_computation | async-start | bytes 1179648 | tf_op jit(solution)/shard_map/all_to_all | solution.py:415
  108.4 16.7 %all-to-all-done = f32[4,384,96]{1,2,0:T(8,128)S(1)} async-done(((f32[4,384,96]{1,2,0:T(8,128)}), f32[4,384,96]{1,2,0:T(8,128)S(1)}, u32[]{:S(2)}, u32[]{:S(2)}) %all-to-all-start) | async-done | bytes 589856 | tf_op jit(solution)/shard_map/all_to_all | solution.py:415
  125.1 1.2 copy.19.own_ref
  126.3 2.7 %gram_step.1 = (f32[384,384]{1,0:T(8,128)}, f32[768,128]{1,0:T(8,128)}) custom-call(s32[1]{0:T(128)} %bitcast.quarter_ref, f32[4,384,96]{2,1,0:T(8,128)} %copy.19.own_ref, f32[1536,128]{1,0:T(8,128)} %get-tuple-element.34.weight_ref), custom_call_target="tpu_custom_call" | custom-call | tf_op jit(solution)/shard_map/gram_step/pallas_call | solution.py:354
  129.0 20.7 %all_to_all.20 = f32[32,24,128]{2,1,0:T(8,128)S(1)} all-to-all(f32[32,24,128]{2,1,0:T(8,128)} %bitcast.8), channel_id=1, replica_groups=mesh['z_hi'=3,'y'=8,'x'=4,'core'=2,'orb'=4] {'x','core','orb'}, dimensions={0} | all-to-all | bytes 786432 | tf_op jit(solution)/shard_map/all_to_all | solution.py:387
  149.8 68.9 %all_to_all.21 = f32[24,24,128]{2,1,0:T(8,128)S(1)} all-to-all(f32[24,24,128]{2,1,0:T(8,128)S(1)} %broadcast_in_dim.4), channel_id=1, replica_groups=mesh['z_hi'=3,'y'=8,'x'=4,'core'=2,'orb'=4] {'z_hi','y'}, dimensions={0} | all-to-all | bytes 589824 | tf_op jit(solution)/shard_map/all_to_all | solution.py:394
  218.8 20.4 %all_to_all.22 = f32[32,24,128]{2,1,0:T(8,128)} all-to-all(f32[32,24,128]{2,1,0:T(8,128)S(1)} %broadcast_in_dim.5), channel_id=1, replica_groups=mesh['z_hi'=3,'y'=8,'x'=4,'core'=2,'orb'=4] {'x','core','orb'}, dimensions={0} | all-to-all | bytes 786432 | tf_op jit(solution)/shard_map/all_to_all | solution.py:400
  239.2 26.9 %rotate_step.1 = f32[1,384,384]{2,1,0:T(8,128)} custom-call(f32[768,128]{1,0:T(8,128)} %bitcast.6, f32[384,384]{1,0:T(8,128)} %get-tuple-element.36.rows_ref), custom_call_target="tpu_custom_call" | custom-call | tf_op jit(solution)/shard_map/rotate_step/pallas_call | solution.py:369
  (4 shorter events, 0.1 us)
Async XLA Ops:
  27.8 14.3 %collective-permute-start = (f32[512,128]{1,0:T(8,128)}, f32[512,128]{1,0:T(8,128)S(1)}, u32[]{:S(2)}, u32[]{:S(2)}) collective-permute-start(f32[512,128]{1,0:T(8,128)} %get-tuple-element.22), channel_id=1, source_target_pairs={{4,0},{8,4},{12,8},{16,12},{20,16},{24,20},{28,24},{32,28},{36,32}... | collective-permute-start | bytes 786440 | tf_op jit(solution)/shard_map/ppermute | solution.py:380
  40.2 5.5 %collective-permute-start.1 = (f32[512,128]{1,0:T(8,128)}, f32[512,128]{1,0:T(8,128)S(1)}, u32[]{:S(2)}, u32[]{:S(2)}) collective-permute-start(f32[512,128]{1,0:T(8,128)} %get-tuple-element.23), channel_id=1, source_target_pairs={{0,4},{4,8},{8,12},{12,16},{16,20},{20,24},{24,28},{28,32},{32,36}... | collective-permute-start | bytes 786440 | tf_op jit(solution)/shard_map/ppermute | solution.py:381
  42.1 3.6 %copy-start = (f32[512,128]{1,0:T(8,128)}, f32[512,128]{1,0:T(8,128)S(1)}, u32[]{:S(2)}) copy-start(f32[512,128]{1,0:T(8,128)S(1)} %collective-permute-done.from_above_ref) | copy-start | bytes 786436
  45.7 0.7 copy-start.1
  60.4 9.9 %collective-permute-start.2 = (f32[512,128]{1,0:T(8,128)}, f32[512,128]{1,0:T(8,128)S(1)}, u32[]{:S(2)}, u32[]{:S(2)}) collective-permute-start(f32[512,128]{1,0:T(8,128)} %get-tuple-element.28), channel_id=1, source_target_pairs={{4,0},{8,4},{12,8},{16,12},{20,16},{24,20},{28,24},{32,28},{36,32}... | collective-permute-start | bytes 786440 | tf_op jit(solution)/shard_map/ppermute | solution.py:380
  62.3 9.2 %collective-permute-start.3 = (f32[512,128]{1,0:T(8,128)}, f32[512,128]{1,0:T(8,128)S(1)}, u32[]{:S(2)}, u32[]{:S(2)}) collective-permute-start(f32[512,128]{1,0:T(8,128)} %get-tuple-element.29), channel_id=1, source_target_pairs={{0,4},{4,8},{8,12},{12,16},{16,20},{20,24},{24,28},{28,32},{32,36}... | collective-permute-start | bytes 786440 | tf_op jit(solution)/shard_map/ppermute | solution.py:381
  70.2 1.3 copy-start.4
  71.5 0.7 copy-start.5
  86.1 9.9 %collective-permute-start.4 = (f32[512,128]{1,0:T(8,128)}, f32[512,128]{1,0:T(8,128)S(1)}, u32[]{:S(2)}, u32[]{:S(2)}) collective-permute-start(f32[512,128]{1,0:T(8,128)} %get-tuple-element.31), channel_id=1, source_target_pairs={{4,0},{8,4},{12,8},{16,12},{20,16},{24,20},{28,24},{32,28},{36,32}... | collective-permute-start | bytes 786440 | tf_op jit(solution)/shard_map/ppermute | solution.py:380
  88.0 9.2 %collective-permute-start.5 = (f32[512,128]{1,0:T(8,128)}, f32[512,128]{1,0:T(8,128)S(1)}, u32[]{:S(2)}, u32[]{:S(2)}) collective-permute-start(f32[512,128]{1,0:T(8,128)} %get-tuple-element.32), channel_id=1, source_target_pairs={{0,4},{4,8},{8,12},{12,16},{16,20},{20,24},{24,28},{28,32},{32,36}... | collective-permute-start | bytes 786440 | tf_op jit(solution)/shard_map/ppermute | solution.py:381
  95.9 1.3 copy-start.2
  97.2 0.7 copy-start.3
  104.9 20.2 %all-to-all-start = ((f32[4,384,96]{1,2,0:T(8,128)}), f32[4,384,96]{1,2,0:T(8,128)S(1)}, u32[]{:S(2)}, u32[]{:S(2)}) async-start(f32[4,384,96]{1,2,0:T(8,128)} %copy.18), calls=%async_computation | async-start | bytes 1179648 | tf_op jit(solution)/shard_map/all_to_all | solution.py:415
